TPU v7x, 32 devices: a whole 2x2x4 slice. The times are simulated.
32 devices in a mesh: row: 4 (over z), col: 8 (over y, x, core).
Axes of the slice: x: 2, y: 2, z: 4, core: 2. Of those that a mesh axis runs over, the one named last changes fastest.
Arguments:
- tokens: bfloat16 [512, 8192], P('col', 'row'), may hold values from -6 to 6
- modality: int32 [512], P('row'), may hold values 0 or 1
- in_weight: bfloat16 [8192, 2, 28672], P('row', None, 'col'), may hold values from -0.0625 to 0.0625
- down_weight: bfloat16 [28672, 8192], P('col', 'row'), may hold values from -0.03125 to 0.03125
- d_mixed: bfloat16 [512, 8192], P('col', 'row'), may hold values from -6 to 6
Outputs:
- mixed: bfloat16 [512, 8192], P('col', 'row')
- d_down: bfloat16 [28672, 8192], P('col', 'row')
- d_in: bfloat16 [8192, 2, 28672], P('row', None, 'col')
- d_tokens: bfloat16 [512, 8192], P('col', 'row')
All inputs are finite; a program needn't handle non-finite values. No bound on the sum of `modality` on one device may be relied on, other than what follows from the above.
Results may differ from a plain program's by a relative error of at most 0.0049.
Values may be sent and summed in bfloat16 or wider, within the bound.
A program may use at most 192 MiB of HBM per device.

v0:
```python
import functools
import math

import jax
import jax.numpy as jnp
from jax import lax
from jax.experimental import pallas as pl
from jax.experimental.pallas import tpu as pltpu
from jax.sharding import PartitionSpec as P

MESH = pl.DeviceIdType.MESH
OVER_LAST = (((1,), (1,)), ((), ()))
OVER_FIRST = (((0,), (0,)), ((), ()))


def dot(a, b, dims=(((1,), (0,)), ((), ()))):
    return lax.dot_general(a, b, dims, preferred_element_type=jnp.float32)


def gather(block, axis):
    count = lax.axis_size(axis)
    me = lax.axis_index(axis)
    out = jnp.zeros((count,) + block.shape, block.dtype)
    out = lax.dynamic_update_index_in_dim(out, block, me, 0)
    for shift in range(1, count):
        moves = [(i, (i + shift) % count) for i in range(count)]
        arrived = lax.ppermute(block, axis, moves)
        out = lax.dynamic_update_index_in_dim(out, arrived, lax.rem(me + count - shift, count), 0)
    return out.reshape((count * block.shape[0],) + block.shape[1:])


def chip_sum(blocks):
    columns = lax.axis_size("col")
    side = math.isqrt(columns // 2)
    total = blocks[0]
    for k in range(1, len(blocks)):
        dy, dx = divmod(k, side)
        moves = [
            (i, ((i // 2 // side + dy) % side * side + (i // 2 + dx) % side) * 2 + i % 2) for i in range(columns)
        ]
        total = total + lax.ppermute(blocks[k], "col", moves).astype(jnp.float32)
    return total


def paired_columns(tile, rows_ref, gate_ref, up_ref, out_ref):
    @pl.loop(0, gate_ref.shape[1] // tile)
    def _(step):
        columns = pl.ds(pl.multiple_of(step * tile, tile), tile)
        for part, side_ref in enumerate((gate_ref, up_ref)):
            out_ref[:, part, columns] = dot(rows_ref[...], side_ref[:, columns], OVER_FIRST).astype(jnp.bfloat16)


def in_gradient(packed, d_gate, d_up):
    depth = packed.shape[2]
    count, width = d_gate.shape
    deep = depth // 8
    tile = max(w for w in range(128, 1025, 128) if width % w == 0)
    return pl.pallas_call(
        functools.partial(paired_columns, tile),
        grid=(depth // deep,),
        in_specs=[
            pl.BlockSpec((None, count, deep), lambda i: (0, 0, i)),
            pl.BlockSpec((count, width), lambda i: (0, 0)),
            pl.BlockSpec((count, width), lambda i: (0, 0)),
        ],
        out_specs=pl.BlockSpec((deep, 2, width), lambda i: (i, 0, 0)),
        out_shape=jax.ShapeDtypeStruct((depth, 2, width), jnp.bfloat16),
        cost_estimate=pl.CostEstimate(
            flops=4 * count * depth * width,
            bytes_accessed=4 * (depth * width + count * width + count * depth),
            transcendentals=0,
        ),
    )(packed, d_gate, d_up)


def swiglu_terms(gate, up, d_hidden):
    sig = jax.nn.sigmoid(gate)
    activated = gate * sig
    d_gate = d_hidden * up * (sig + gate * sig * (1.0 - sig))
    return activated * up, d_gate, d_hidden * activated


def gather_kernel(
    size, side, tokens_ref, modality_ref, d_mixed_ref, packed_ref, pick_ref, count_ref,
    whole, chosen, local_sem, mate_send, mate_recv, send, recv, row_send, row_recv, hand_send, hand_recv,
):
    z, column = lax.axis_index("row"), lax.axis_index("col")
    core, chip = lax.rem(column, 2), column // 2
    y, x = chip // side, lax.rem(chip, side)
    rows = tokens_ref.shape[0]
    chips = side * side

    def at(part):
        return whole.at[pl.ds(pl.multiple_of(part * rows, rows), rows), :]

    def remote(src, dst, send_sem, recv_sem, where):
        return pltpu.make_async_remote_copy(
            src_ref=src, dst_ref=dst, send_sem=send_sem, recv_sem=recv_sem, device_id=where, device_id_type=MESH
        )

    def chip_of(dy, dx):
        return lax.rem(y + dy, side) * side + lax.rem(x + dx, side)

    mate = {"col": chip * 2 + 1 - core}
    others = [(dy, dx) for dy in range(side) for dx in range(side) if dy or dx]
    if side == 2:
        straight = [(0, 1), (1, 0)]
    else:
        straight = others

    def block_copy(k, source, half, dy, dx):
        part = source * 2 + half
        return remote(at(part), at(part), send.at[k], recv.at[part], {"col": chip_of(dy, dx) * 2 + core})

    def arrival(part):
        return remote(at(part), at(part), send.at[0], recv.at[part], mate)

    barrier = pltpu.get_barrier_semaphore()
    pl.semaphore_signal(barrier, inc=1, device_id=mate, device_id_type=MESH)
    for dy, dx in straight:
        pl.semaphore_signal(
            barrier, inc=1, device_id={"col": chip_of(dy, dx) * 2 + core}, device_id_type=MESH
        )
    for step in range(1, size):
        pl.semaphore_signal(barrier, inc=1, device_id={"row": lax.rem(z + step, size)}, device_id_type=MESH)
    mine = chip * 2 + core
    for k, (kept, given) in enumerate(((tokens_ref, d_mixed_ref), (d_mixed_ref, tokens_ref))):
        @pl.when(core == k)
        def _():
            pltpu.make_async_copy(kept, at(mine), local_sem.at[0]).start()

    pltpu.make_async_copy(modality_ref, chosen.at[z], local_sem.at[1]).start()
    pl.semaphore_wait(barrier, len(straight) + size)

    def mate_copy(given):
        return remote(given, at(mine), mate_send, mate_recv, mate)

    for k, given in enumerate((d_mixed_ref, tokens_ref)):
        @pl.when(core == k)
        def _():
            mate_copy(given).start()

    row_copies = [
        remote(
            modality_ref, chosen.at[z], row_send.at[step - 1], row_recv.at[step - 1],
            {"row": lax.rem(z + step, size)},
        )
        for step in range(1, size)
    ]
    for copy in row_copies:
        copy.start()
    pltpu.make_async_copy(tokens_ref, at(mine), local_sem.at[0]).wait()
    first = [block_copy(k, chip, core, dy, dx) for k, (dy, dx) in enumerate(straight)]
    for copy in first:
        copy.start()
    mate_copy(tokens_ref).wait_recv()
    base = len(straight)
    second = [block_copy(base + k, chip, 1 - core, dy, dx) for k, (dy, dx) in enumerate(straight)]
    for copy in second:
        copy.start()
    relays = []
    if side == 2:
        arrival(chip_of(0, 1) * 2).wait_recv()
        relays.append(block_copy(2 * base, chip_of(0, 1), 0, 1, 0))
        relays[-1].start()
        arrival(chip_of(1, 0) * 2 + 1).wait_recv()
        relays.append(block_copy(2 * base + 1, chip_of(1, 0), 1, 0, 1))
        relays[-1].start()

    pltpu.make_async_copy(modality_ref, chosen.at[z], local_sem.at[1]).wait()
    for copy in row_copies:
        copy.wait_recv()
    total = whole.shape[0]
    picked = jnp.concatenate([chosen[k] for k in range(size)], axis=1) == 1
    ones = jnp.broadcast_to(picked.astype(jnp.float32), (8, total))
    up_to = lax.broadcasted_iota(jnp.int32, (total, total), 0) <= lax.broadcasted_iota(
        jnp.int32, (total, total), 1
    )
    running = dot(ones.astype(jnp.bfloat16), up_to.astype(jnp.float32).astype(jnp.bfloat16))
    place = jnp.where(ones > 0.5, running, 0.0)[:1].astype(jnp.int32) - 1
    slot = lax.broadcasted_iota(jnp.int32, pick_ref.shape, 0)
    pick_ref[...] = (slot == place).astype(jnp.float32).astype(jnp.bfloat16)
    count_ref[...] = jnp.broadcast_to(jnp.sum(ones[:1], axis=1, keepdims=True), count_ref.shape)

    if side == 2:
        rest = [
            (chip_of(0, 1), 1), (chip_of(1, 0), 0), (chip_of(1, 1), 0), (chip_of(1, 1), 1),
        ]
    else:
        rest = [(chip_of(dy, dx), half) for dy, dx in others for half in range(2)]
    for source, half in rest:
        arrival(source * 2 + half).wait_recv()
    packed_ref[core] = dot(pick_ref[...], whole[...]).astype(jnp.bfloat16)
    hand = remote(packed_ref.at[core], packed_ref.at[core], hand_send, hand_recv, mate)
    hand.start()
    for copy in first + second + relays + row_copies:
        copy.wait_send()
    mate_copy(tokens_ref).wait_send()
    hand.wait_send()
    remote(packed_ref.at[1 - core], packed_ref.at[1 - core], hand_send, hand_recv, mate).wait_recv()


def gather_packed(tokens, modality, d_mixed, packed, collective_id):
    size, columns = lax.axis_size("row"), lax.axis_size("col")
    side = math.isqrt(columns // 2)
    rows, depth = tokens.shape
    total = rows * columns
    sends = 6 if side == 2 else 2 * (side * side - 1)
    vmem = pl.BlockSpec(memory_space=pltpu.VMEM)
    dma = pltpu.SemaphoreType.DMA
    return pl.pallas_call(
        functools.partial(gather_kernel, size, side),
        in_specs=[vmem] * 3,
        out_specs=[vmem] * 3,
        out_shape=[
            jax.ShapeDtypeStruct((2, packed, depth), jnp.bfloat16),
            jax.ShapeDtypeStruct((packed, total), jnp.bfloat16),
            jax.ShapeDtypeStruct((8, 128), jnp.float32),
        ],
        scratch_shapes=[
            pltpu.VMEM((total, depth), jnp.bfloat16),
            pltpu.VMEM((size, 1, total // size), jnp.int32),
            dma((2,)), dma, dma, dma((sends,)), dma((columns,)), dma((size - 1,)), dma((size - 1,)), dma, dma,
        ],
        compiler_params=pltpu.CompilerParams(collective_id=collective_id, has_side_effects=True),
        cost_estimate=pl.CostEstimate(
            flops=2 * packed * total * depth, bytes_accessed=4 * total * depth, transcendentals=0
        ),
    )(tokens, modality.reshape(1, -1), d_mixed)


def unpack(pairs_ref, columns_ref, apart):
    depth, _, wide = pairs_ref.shape
    tall = apart.shape[1] // 2
    buffers = apart.shape[0]

    @pl.loop(0, depth // (tall * buffers))
    def _(step):
        for buffer in range(buffers):
            rows = pl.ds(pl.multiple_of((step * buffers + buffer) * tall, tall), tall)
            apart[buffer] = pairs_ref[rows].reshape(2 * tall, wide).astype(jnp.float32)
            for part in range(2):
                one = apart[buffer, pl.ds(part, tall, stride=2), :]
                columns_ref[rows, part * wide:(part + 1) * wide] = one.astype(jnp.bfloat16)


def chain_kernel(
    size, side, units, wide, packed_ref, pick_ref, in_ref, down_ref, hidden_ref, d_gate_ref, d_up_ref, own_ref, *rest
):
    other_refs, scratch = rest[:side * side - 1], rest[side * side - 1:]
    (
        total_ref, pick_rows, mine, given, got, raw, apart, w_down, w_in, partial, sums, terms,
        load_sem, sum_send, sum_recv, term_send, term_recv, out_sem, pair_send, pair_recv,
    ) = scratch
    z, column = lax.axis_index("row"), lax.axis_index("col")
    core, chip = lax.rem(column, 2), column // 2
    mate = {"col": chip * 2 + 1 - core}
    shifts = [(dy, dx) for dy in range(side) for dx in range(side)]
    middle = size // 2
    slots = w_down.shape[0]
    held = partial.shape[0]
    near = jnp.minimum(z, size - 1 - z)
    count = partial.shape[1]
    cut = count // 16 * 8
    spans = (slice(0, cut), slice(cut, count))

    def owner_of(u):
        return middle - 1 + lax.rem(u, 2)

    def loads(u):
        columns = pl.ds(pl.multiple_of(u * wide, wide), wide)
        slot = lax.rem(u, 2)
        return (
            pltpu.make_async_copy(in_ref.at[:, :, columns], raw.at[slot], load_sem.at[0, slot]),
            pltpu.make_async_copy(down_ref.at[columns, :], w_down.at[lax.rem(u, slots)], load_sem.at[1, slot]),
        )

    def sum_copy(u, side, h):
        return pltpu.make_async_remote_copy(
            src_ref=sums.at[side, u, spans[h]], dst_ref=sums.at[side, u, spans[h]],
            send_sem=sum_send.at[h, u], recv_sem=sum_recv.at[h, side, u],
            device_id={"row": z + 1 - 2 * side}, device_id_type=MESH,
        )

    def term_copy(u, side, h):
        return pltpu.make_async_remote_copy(
            src_ref=terms.at[u, spans[h]], dst_ref=terms.at[u, spans[h]],
            send_sem=term_send.at[h, side, u], recv_sem=term_recv.at[h, u],
            device_id={"row": z + 1 - 2 * side}, device_id_type=MESH,
        )

    def out_copies(u):
        columns = pl.ds(pl.multiple_of(u * wide, wide), wide)
        return [
            pltpu.make_async_copy(
                terms.at[u, :, k * wide:(k + 1) * wide], ref.at[:, columns], out_sem.at[k, u]
            )
            for k, ref in enumerate((hidden_ref, d_gate_ref, d_up_ref))
        ]

    barrier = pltpu.get_barrier_semaphore()
    for step in (-1, 1):
        @pl.when((z + step >= 0) & (z + step < size))
        def _():
            pl.semaphore_signal(barrier, inc=1, device_id={"row": z + step}, device_id_type=MESH)
    pl.semaphore_signal(barrier, inc=1, device_id=mate, device_id_type=MESH)
    for copy in loads(0):
        copy.start()
    @pl.loop(0, count // 8)
    def _(step):
        total_ref[pl.ds(pl.multiple_of(step * 8, 8), 8), :] = jnp.zeros((8, total_ref.shape[1]), jnp.float32)

    depth = down_ref.shape[1]
    rows = own_ref.shape[0]
    same = lax.broadcasted_iota(jnp.int32, (count, count), 0) == lax.broadcasted_iota(jnp.int32, (count, count), 1)
    turned = dot(pick_ref[:count], same.astype(jnp.float32).astype(jnp.bfloat16), OVER_FIRST)
    pick_rows[...] = turned.astype(jnp.bfloat16)
    pl.semaphore_wait(barrier, jnp.where(near > 0, 3, 2))

    @pl.loop(0, units + 2 * middle + 3)
    def _(t):
        @pl.when(t < units)
        def _():
            for copy in loads(t):
                copy.wait()

            @pl.when(t + 1 < units)
            def _():
                for copy in loads(t + 1):
                    copy.start()

            slot, here = lax.rem(t, slots), lax.rem(t, held)
            unpack(raw.at[lax.rem(t, 2)], w_in.at[slot], apart)
            partial[here, :, :2 * wide] = dot(packed_ref[0, :count], w_in[slot])
            partial[here, :, 2 * wide:] = dot(packed_ref[1, :count], w_down[slot], OVER_LAST)

        relayed = t - near

        @pl.when((relayed >= 0) & (relayed < units) & (owner_of(relayed) != z))
        def _():
            side = jnp.where(z < owner_of(relayed), 0, 1)
            here = lax.rem(relayed, held)
            for h, span in enumerate(spans):
                @pl.when(near > 0)
                def _():
                    sum_copy(relayed, side, h).wait_recv()
                    sums[side, relayed, span] = (
                        partial[here, span] + sums[side, relayed, span].astype(jnp.float32)
                    ).astype(sums.dtype)

                @pl.when(near == 0)
                def _():
                    sums[side, relayed, span] = partial[here, span].astype(sums.dtype)

                sum_copy(relayed, side, h).start()

        closed = t - middle

        @pl.when((closed >= 0) & (closed < units) & (owner_of(closed) == z))
        def _():
            here = lax.rem(closed, held)
            for h, span in enumerate(spans):
                @pl.when(z > 0)
                def _():
                    sum_copy(closed, 0, h).wait_recv()
                    partial[here, span] += sums[0, closed, span].astype(jnp.float32)

                @pl.when(z < size - 1)
                def _():
                    sum_copy(closed, 1, h).wait_recv()
                    partial[here, span] += sums[1, closed, span].astype(jnp.float32)

                results = swiglu_terms(*(partial[here, span, k * wide:(k + 1) * wide] for k in range(3)))
                for k, result in enumerate(results):
                    terms[closed, span, k * wide:(k + 1) * wide] = result.astype(jnp.bfloat16)

                @pl.when(z < size - 1)
                def _():
                    term_copy(closed, 0, h).start()

                @pl.when(z > 0)
                def _():
                    term_copy(closed, 1, h).start()

        passed = t - (2 * middle + 2 - near)

        @pl.when((passed >= 0) & (passed < units) & (owner_of(passed) != z) & (near > 0))
        def _():
            side = jnp.where(z < owner_of(passed), 1, 0)
            for h in range(2):
                term_copy(passed, side, h).wait_recv()
                term_copy(passed, side, h).start()

        used = t - (2 * middle + 3 - near)

        @pl.when((used >= 0) & (used < units))
        def _():
            @pl.when((owner_of(used) != z) & (near == 0))
            def _():
                for h in range(2):
                    term_copy(used, 0, h).wait_recv()

            for copy in out_copies(used):
                copy.start()
            slot = lax.rem(used, slots)
            total_ref[:, :depth] += dot(terms[used, :, :wide], w_down[slot])
            total_ref[:, depth:] += dot(terms[used, :, wide:], w_in[slot], OVER_LAST)

    span = mine.shape[2]

    def pair_copy(b):
        return pltpu.make_async_remote_copy(
            src_ref=given.at[b], dst_ref=got.at[b], send_sem=pair_send.at[b], recv_sem=pair_recv.at[b],
            device_id=mate, device_id_type=MESH,
        )

    def chosen_rows(which):
        parts = []
        for dy, dx in shifts:
            there = lax.rem(chip // side + dy, side) * side + lax.rem(lax.rem(chip, side) + dx, side)
            start = pl.multiple_of((there * 2 + which) * rows, rows)
            parts.append(pick_rows[pl.ds(start, rows), :])
        return jnp.concatenate(parts, axis=0)

    ours, theirs = chosen_rows(core), chosen_rows(1 - core)

    @pl.loop(0, mine.shape[0])
    def _(b):
        part = total_ref[:, pl.ds(pl.multiple_of(b * span, span), span)]
        high = part.astype(jnp.bfloat16)
        low = (part - high.astype(jnp.float32)).astype(jnp.bfloat16)
        given[b] = (dot(theirs, high) + dot(theirs, low)).astype(jnp.bfloat16)
        pair_copy(b).start()
        mine[b] = dot(ours, high) + dot(ours, low)

    @pl.loop(0, mine.shape[0])
    def _(b):
        pair_copy(b).wait_recv()
        columns = pl.ds(pl.multiple_of(b * span, span), span)
        both = mine[b] + got[b].astype(jnp.float32)
        for k, ref in enumerate((own_ref,) + tuple(other_refs)):
            ref[:, columns] = both[k * rows:(k + 1) * rows].astype(ref.dtype)

    @pl.loop(0, mine.shape[0])
    def _(b):
        pair_copy(b).wait_send()

    @pl.loop(0, units)
    def _(u):
        owner = owner_of(u)
        for copy in out_copies(u):
            copy.wait()

        @pl.when(owner != z)
        def _():
            for h in range(2):
                sum_copy(u, jnp.where(z < owner, 0, 1), h).wait_send()

            @pl.when(near > 0)
            def _():
                for h in range(2):
                    term_copy(u, jnp.where(z < owner, 1, 0), h).wait_send()

        @pl.when(owner == z)
        def _():
            @pl.when(z < size - 1)
            def _():
                for h in range(2):
                    term_copy(u, 0, h).wait_send()

            @pl.when(z > 0)
            def _():
                for h in range(2):
                    term_copy(u, 1, h).wait_send()


def chain(packed, pick, count, in_weight, down_weight, collective_id):
    size, columns = lax.axis_size("row"), lax.axis_size("col")
    side = math.isqrt(columns // 2)
    chips, rows = side * side, pick.shape[1] // columns
    blocks = 8
    depth = packed.shape[2]
    width = down_weight.shape[0]
    wide = 128
    units = width // wide
    slots = 2 * (size // 2) + 6
    held = size // 2 + 1
    sum_type = jnp.bfloat16 if size <= 4 else jnp.float32
    vmem, hbm = pl.BlockSpec(memory_space=pltpu.VMEM), pl.BlockSpec(memory_space=pl.ANY)
    dma = pltpu.SemaphoreType.DMA
    return pl.pallas_call(
        functools.partial(chain_kernel, size, side, units, wide),
        in_specs=[vmem, vmem, hbm, hbm],
        out_specs=[hbm] * 3 + [vmem] * chips,
        out_shape=[jax.ShapeDtypeStruct((count, width), jnp.bfloat16)] * 3
        + [jax.ShapeDtypeStruct((rows, 2 * depth), jnp.float32)]
        + [jax.ShapeDtypeStruct((rows, 2 * depth), jnp.bfloat16)] * (chips - 1),
        scratch_shapes=[
            pltpu.VMEM((count, 2 * depth), jnp.float32),
            pltpu.VMEM((pick.shape[1], count), jnp.bfloat16),
            pltpu.VMEM((blocks, chips * rows, 2 * depth // blocks), jnp.float32),
            pltpu.VMEM((blocks, chips * rows, 2 * depth // blocks), jnp.bfloat16),
            pltpu.VMEM((blocks, chips * rows, 2 * depth // blocks), jnp.bfloat16),
            pltpu.VMEM((2, depth, 2, wide), jnp.bfloat16),
            pltpu.VMEM((8, 128, wide), jnp.float32),
            pltpu.VMEM((slots, wide, depth), jnp.bfloat16),
            pltpu.VMEM((slots, depth, 2 * wide), jnp.bfloat16),
            pltpu.VMEM((held, count, 3 * wide), jnp.float32),
            pltpu.VMEM((2, units, count, 3 * wide), sum_type),
            pltpu.VMEM((units, count, 3 * wide), jnp.bfloat16),
            dma((2, 2)), dma((2, units)), dma((2, 2, units)), dma((2, 2, units)), dma((2, units)), dma((3, units)),
            dma((blocks,)), dma((blocks,)),
        ],
        compiler_params=pltpu.CompilerParams(
            collective_id=collective_id, has_side_effects=True, vmem_limit_bytes=60 * 1024 * 1024
        ),
        cost_estimate=pl.CostEstimate(
            flops=12 * count * depth * width, bytes_accessed=6 * depth * width, transcendentals=count * width
        ),
    )(packed, pick, in_weight, down_weight)


def per_device(tokens, modality, in_weight, down_weight, d_mixed):
    total = tokens.shape[0] * lax.axis_size("col")
    depth = tokens.shape[1]
    rooms = (total // 2, total * 9 // 16)
    packed, pick, count = gather_packed(tokens, modality, d_mixed, rooms[-1], 1)

    def gradients(packed, hidden, d_gate, d_up, blocks):
        mine = chip_sum(blocks).astype(jnp.bfloat16)
        d_down = dot(hidden, packed[1, :hidden.shape[0]], OVER_FIRST).astype(jnp.bfloat16)
        return (mine[:, :depth], d_down, in_gradient(packed, d_gate, d_up), mine[:, depth:])

    def packed_form(room, collective_id, packed, pick, tokens, modality, d_mixed, w_in, w_down):
        hidden, d_gate, d_up, *blocks = chain(packed, pick, room, w_in, w_down, collective_id)
        return gradients(packed, hidden, d_gate, d_up, blocks)

    def whole_form(packed, pick, tokens, modality, d_mixed, w_in, w_down):
        keep = (gather(modality, "row") == 1)[:, None].astype(jnp.bfloat16)
        both = gather(jnp.concatenate([tokens, d_mixed], 1), "col") * keep
        both = both.reshape(total, 2, depth).transpose(1, 0, 2)
        room = total // 2

        def half_of(k):
            part = lax.dynamic_slice_in_dim(both, k * room, room, 1)
            spots = jnp.arange(room)[:, None] + k * room == jnp.arange(total)[None, :]
            return chain(part, spots.astype(jnp.bfloat16), room, w_in, w_down, 2 + len(rooms))

        outs = lax.map(lambda k: lax.optimization_barrier(half_of(k)), jnp.arange(2))
        hidden, d_gate, d_up = (x.reshape(total, -1) for x in outs[:3])
        return gradients(both, hidden, d_gate, d_up, [x[0] + x[1] for x in outs[3:]])

    forms = [functools.partial(packed_form, room, 2 + k) for k, room in enumerate(rooms)] + [whole_form]
    chosen = sum((count[0, 0] > room).astype(jnp.int32) for room in rooms)
    return lax.switch(chosen, forms, packed, pick, tokens, modality, d_mixed, in_weight, down_weight)


def solution(mesh):
    return jax.shard_map(
        per_device,
        mesh=mesh,
        in_specs=(
            P("col", "row"),
            P("row"),
            P("row", None, "col"),
            P("col", "row"),
            P("col", "row"),
        ),
        out_specs=(P("col", "row"), P("col", "row"), P("row", None, "col"), P("col", "row")),
        check_vma=False,
    )
```

profile of v0, /device:TPU:0, one launch (start us, length us, event | category | flops | bytes accessed | tf_op | source)
XLA Modules:
  0.0 229.3 jit_solution(3870087959687835181)
XLA Ops:
  0.6 29.3 %shard_map.84 = (bf16[2,288,2048]{2,1,0:T(8,128)(2,1)S(1)}, bf16[288,512]{1,0:T(8,128)(2,1)S(1)}, f32[8,128]{1,0:T(8,128)}) custom-call(bf16[64,2048]{1,0:T(8,128)(2,1)} %tokens_ref.1, s32[1,128]{1,0:T(1,128)} %bitcast.82, bf16[64,2048]{1,0:T(8,128)(2,1)} %d_mixed_ref.1), custom_call_target="tpu_custom_call" | custom-call | flops 603979776 | bytes 4194304 | tf_op jit(solution)/shard_map/pallas_call | solution.py:211
  30.0 1.2 slice.55
  32.5 196.8 %conditional.2 = (bf16[64,2048]{1,0:T(8,128)(2,1)}, bf16[3584,2048]{1,0:T(8,128)(2,1)}, bf16[2048,2,3584]{2,1,0:T(2,128)(2,1)}, bf16[64,2048]{1,0:T(8,128)(2,1)}) conditional(s32[]{:T(128)} %bitcast.33, (bf16[2,288,2048]{2,1,0:T(8,128)(2,1)S(1)}, bf16[288,512]{1,0:T(8,128)(2,1)S(1)}, bf16[2048,2,3584]{2,1,0:T(2,128)(2,1)}, ...), branch_computations={%region_0.0_spmd, %region_1.0_spmd, %region_2.5_spmd} | conditional | flops 45102399488 | bytes 227301760
  32.5 156.1 %branch_0_fun.2 = (bf16[256,3584]{1,0:T(8,128)(2,1)}, bf16[256,3584]{1,0:T(8,128)(2,1)}, bf16[256,3584]{1,0:T(8,128)(2,1)}, f32[64,4096]{1,0:T(8,128)}, bf16[64,...) custom-call(bf16[2,288,2048]{2,1,0:T(8,128)(2,1)S(1)} %get-tuple-element.79.packed_ref.rows_ref, ...), custom_call_target="tpu_custom_call" | custom-call | flops 22548578304 | bytes 44040192 | tf_op jit(solution)/shard_map/cond/branch_0_fun/pallas_call | solution.py:491
  188.6 2.8 %collective-permute-start = (bf16[64,4096]{1,0:T(8,128)(2,1)}, bf16[64,4096]{1,0:T(8,128)(2,1)}, u32[]{:S(2)}, u32[]{:S(2)}) collective-permute-start(bf16[64,4096]{1,0:T(8,128)(2,1)} %get-tuple-element.84), channel_id=1, source_target_pairs={{0,2},{1,3},{2,0},{3,1},{4,6},{5,7},{6,4},{7,5},{8,10},{9,11},{10,... | collective-permute-start | bytes 1572872 | tf_op jit(solution)/shard_map/cond/branch_0_fun/ppermute | solution.py:41
  191.4 1.5 collective-permute-start.1
  192.9 0.0 collective-permute-start.2
  193.0 9.1 %fusion = bf16[3584,2048]{1,0:T(8,128)(2,1)} fusion(bf16[256,3584]{1,0:T(8,128)(2,1)} %get-tuple-element.87, bf16[2,288,2048]{2,1,0:T(8,128)(2,1)S(1)} %get-tuple-element.79.packed_ref.rows_ref), kind=kOutput, calls=%fused_computation | convolution fusion | flops 3758096384 | bytes 17563648 | tf_op jit(solution)/shard_map/cond/branch_0_fun/dot_general | solution.py:17
  202.1 0.0 copy-start.5
  202.1 24.8 %branch_0_fun.3 = bf16[2048,2,3584]{2,1,0:T(2,128)(2,1)} custom-call(bf16[2,288,2048]{2,1,0:T(8,128)(2,1)S(1)} %get-tuple-element.79.packed_ref.rows_ref, bf16[256,3584]{1,0:T(8,128)(2,1)} %get-tuple-element.88.gate_ref, bf16[256,3584]{1,0:T(8,128)(2,1)} %get-tuple-element.89.up_ref), custom_call_target="tpu_custom_call" | custom-call | flops 7516192768 | bytes 35127296 | tf_op jit(solution)/shard_map/cond/branch_0_fun/pallas_call | solution.py:58
  226.8 0.0 collective-permute-done
  226.8 0.0 collective-permute-done.1
  226.8 0.0 collective-permute-done.2
  226.9 0.0 copy-done.5
  226.9 1.6 add_convert_fusion
  228.5 0.8 fusion.13
Async XLA Ops:
  188.6 38.2 %collective-permute-start = (bf16[64,4096]{1,0:T(8,128)(2,1)}, bf16[64,4096]{1,0:T(8,128)(2,1)}, u32[]{:S(2)}, u32[]{:S(2)}) collective-permute-start(bf16[64,4096]{1,0:T(8,128)(2,1)} %get-tuple-element.84), channel_id=1, source_target_pairs={{0,2},{1,3},{2,0},{3,1},{4,6},{5,7},{6,4},{7,5},{8,10},{9,11},{10,... | collective-permute-start | bytes 1572872 | tf_op jit(solution)/shard_map/cond/branch_0_fun/ppermute | solution.py:41
  191.4 35.4 %collective-permute-start.1 = (bf16[64,4096]{1,0:T(8,128)(2,1)}, bf16[64,4096]{1,0:T(8,128)(2,1)}, u32[]{:S(2)}, u32[]{:S(2)}) collective-permute-start(bf16[64,4096]{1,0:T(8,128)(2,1)} %get-tuple-element.85), channel_id=1, source_target_pairs={{0,4},{1,5},{2,6},{3,7},{4,0},{5,1},{6,2},{7,3},{8,12},{9,13},{10,... | collective-permute-start | bytes 1572872 | tf_op jit(solution)/shard_map/cond/branch_0_fun/ppermute | solution.py:41
  192.9 33.9 %collective-permute-start.2 = (bf16[64,4096]{1,0:T(8,128)(2,1)}, bf16[64,4096]{1,0:T(8,128)(2,1)}, u32[]{:S(2)}, u32[]{:S(2)}) collective-permute-start(bf16[64,4096]{1,0:T(8,128)(2,1)} %get-tuple-element.86), channel_id=1, source_target_pairs={{0,6},{1,7},{2,4},{3,5},{4,2},{5,3},{6,0},{7,1},{8,14},{9,15},{10,... | collective-permute-start | bytes 1572872 | tf_op jit(solution)/shard_map/cond/branch_0_fun/ppermute | solution.py:41
  202.1 24.8 %copy-start.5 = (f32[64,4096]{1,0:T(8,128)S(1)}, f32[64,4096]{1,0:T(8,128)}, u32[]{:S(2)}) copy-start(f32[64,4096]{1,0:T(8,128)} %get-tuple-element.83) | copy-start | bytes 3145732 | tf_op jit(solution)/shard_map/conditional
where the time goes:
time: 230 us; the launch traced here: 229 us
  Pallas kernels  210 us (91%)
  matrix products  9.07 us (4%)
  starting transfers between devices  4.35 us (2%)
    pallas_call x1, Pallas kernels, chain(): pl.pallas_call(functools.partial(chain_kernel, size, side, units, wide),...  156 us
    pallas_call x1, Pallas kernels, gather_packed(): pl.pallas_call(functools.partial(gather_kernel, size, side), in_specs=[vm...  29.3 us
    pallas_call x1, Pallas kernels, in_gradient(): pl.pallas_call(functools.partial(paired_columns, tile), grid=(depth // de...  24.8 us
    dot_general x1, matrix products, dot(): return lax.dot_general(a, b, dims, preferred_element_type=jnp.float32)  9.07 us
  transfers between devices with their start and end apart: 3, of which 0 were waited for; matrix products, arithmetic and copies ran while one was open for 4% of the time, Pallas kernels for 11%

commit v1 on v0

--- a/solution.py
+++ b/solution.py
@@ -43,18 +43,23 @@
 
 
 def paired_columns(tile, rows_ref, gate_ref, up_ref, out_ref):
-    @pl.loop(0, gate_ref.shape[1] // tile)
-    def _(step):
-        columns = pl.ds(pl.multiple_of(step * tile, tile), tile)
+    def some(columns):
         for part, side_ref in enumerate((gate_ref, up_ref)):
             out_ref[:, part, columns] = dot(rows_ref[...], side_ref[:, columns], OVER_FIRST).astype(jnp.bfloat16)
 
-
-def in_gradient(packed, d_gate, d_up):
+    if tile == gate_ref.shape[1]:
+        some(slice(None))
+    else:
+        pl.loop(0, gate_ref.shape[1] // tile)(
+            lambda step: some(pl.ds(pl.multiple_of(step * tile, tile), tile))
+        )
+
+
+def in_gradient(packed, d_gate, d_up, widest):
     depth = packed.shape[2]
     count, width = d_gate.shape
     deep = depth // 8
-    tile = max(w for w in range(128, 1025, 128) if width % w == 0)
+    tile = max(w for w in range(128, min(width, widest) + 1, 128) if width % w == 0)
     return pl.pallas_call(
         functools.partial(paired_columns, tile),
         grid=(depth // deep,),
@@ -232,16 +237,12 @@
 def unpack(pairs_ref, columns_ref, apart):
     depth, _, wide = pairs_ref.shape
     tall = apart.shape[1] // 2
-    buffers = apart.shape[0]
-
-    @pl.loop(0, depth // (tall * buffers))
-    def _(step):
-        for buffer in range(buffers):
-            rows = pl.ds(pl.multiple_of((step * buffers + buffer) * tall, tall), tall)
-            apart[buffer] = pairs_ref[rows].reshape(2 * tall, wide).astype(jnp.float32)
-            for part in range(2):
-                one = apart[buffer, pl.ds(part, tall, stride=2), :]
-                columns_ref[rows, part * wide:(part + 1) * wide] = one.astype(jnp.bfloat16)
+    for step in range(depth // tall):
+        rows, buffer = slice(step * tall, (step + 1) * tall), step % apart.shape[0]
+        apart[buffer] = pairs_ref[rows].reshape(2 * tall, wide).astype(jnp.float32)
+        for part in range(2):
+            one = apart[buffer, pl.ds(part, tall, stride=2), :]
+            columns_ref[rows, part * wide:(part + 1) * wide] = one.astype(jnp.bfloat16)
 
 
 def chain_kernel(
@@ -526,14 +527,14 @@
     rooms = (total // 2, total * 9 // 16)
     packed, pick, count = gather_packed(tokens, modality, d_mixed, rooms[-1], 1)
 
-    def gradients(packed, hidden, d_gate, d_up, blocks):
+    def gradients(packed, hidden, d_gate, d_up, blocks, widest):
         mine = chip_sum(blocks).astype(jnp.bfloat16)
         d_down = dot(hidden, packed[1, :hidden.shape[0]], OVER_FIRST).astype(jnp.bfloat16)
-        return (mine[:, :depth], d_down, in_gradient(packed, d_gate, d_up), mine[:, depth:])
+        return (mine[:, :depth], d_down, in_gradient(packed, d_gate, d_up, widest), mine[:, depth:])
 
     def packed_form(room, collective_id, packed, pick, tokens, modality, d_mixed, w_in, w_down):
         hidden, d_gate, d_up, *blocks = chain(packed, pick, room, w_in, w_down, collective_id)
-        return gradients(packed, hidden, d_gate, d_up, blocks)
+        return gradients(packed, hidden, d_gate, d_up, blocks, 4096)
 
     def whole_form(packed, pick, tokens, modality, d_mixed, w_in, w_down):
         keep = (gather(modality, "row") == 1)[:, None].astype(jnp.bfloat16)
@@ -548,7 +549,7 @@
 
         outs = lax.map(lambda k: lax.optimization_barrier(half_of(k)), jnp.arange(2))
         hidden, d_gate, d_up = (x.reshape(total, -1) for x in outs[:3])
-        return gradients(both, hidden, d_gate, d_up, [x[0] + x[1] for x in outs[3:]])
+        return gradients(both, hidden, d_gate, d_up, [x[0] + x[1] for x in outs[3:]], 512)
 
     forms = [functools.partial(packed_form, room, 2 + k) for k, room in enumerate(rooms)] + [whole_form]
     chosen = sum((count[0, 0] > room).astype(jnp.int32) for room in rooms)

time: 230 us -> 220 us (0.957)
  Pallas kernels: 210 us -> 201 us
    pallas_call x1, Pallas kernels: 24.8 us -> 18.9 us  [in_gradient(): pl.pallas_call(functools.partial(paired_columns, tile), grid=(depth // de...]
    pallas_call x1, Pallas kernels: 156 us -> 153 us  [chain(): pl.pallas_call(functools.partial(chain_kernel, size, side, units, wide),...]
  transfers between devices with their start and end apart: 3 -> 3, of which waited for: 0 -> 0; matrix products, arithmetic and copies ran while one was open for 4% -> 4% of each run, Pallas kernels for 11% -> 9%
where the time goes in v1:
time: 220 us
  Pallas kernels  201 us (91%)
  matrix products  9.07 us (4%)
  starting transfers between devices  3.55 us (2%)
    pallas_call x1, Pallas kernels, chain(): pl.pallas_call(functools.partial(chain_kernel, size, side, units, wide),...  153 us
    pallas_call x1, Pallas kernels, gather_packed(): pl.pallas_call(functools.partial(gather_kernel, size, side), in_specs=[vm...  29.3 us
    pallas_call x1, Pallas kernels, in_gradient(): pl.pallas_call(functools.partial(paired_columns, tile), grid=(depth // de...  18.9 us
    dot_general x1, matrix products, dot(): return lax.dot_general(a, b, dims, preferred_element_type=jnp.float32)  9.07 us
  transfers between devices with their start and end apart: 3, of which 0 were waited for; matrix products, arithmetic and copies ran while one was open for 4% of the time, Pallas kernels for 9%

profile of v1, /device:TPU:0, one launch (start us, length us, event | category | flops | bytes accessed | tf_op | source)
XLA Modules:
  0.0 219.6 jit_solution(16596816305808117452)
XLA Ops:
  0.6 29.3 %shard_map.84 = (bf16[2,288,2048]{2,1,0:T(8,128)(2,1)S(1)}, bf16[288,512]{1,0:T(8,128)(2,1)S(1)}, f32[8,128]{1,0:T(8,128)}) custom-call(bf16[64,2048]{1,0:T(8,128)(2,1)} %tokens_ref.1, s32[1,128]{1,0:T(1,128)} %bitcast.82, bf16[64,2048]{1,0:T(8,128)(2,1)} %d_mixed_ref.1), custom_call_target="tpu_custom_call" | custom-call | flops 603979776 | bytes 4194304 | tf_op jit(solution)/shard_map/pallas_call | solution.py:216
  30.0 1.2 slice.55
  32.5 187.1 %conditional.2 = (bf16[64,2048]{1,0:T(8,128)(2,1)}, bf16[3584,2048]{1,0:T(8,128)(2,1)}, bf16[2048,2,3584]{2,1,0:T(2,128)(2,1)}, bf16[64,2048]{1,0:T(8,128)(2,1)}) conditional(s32[]{:T(128)} %bitcast.33, (bf16[2,288,2048]{2,1,0:T(8,128)(2,1)S(1)}, bf16[288,512]{1,0:T(8,128)(2,1)S(1)}, bf16[2048,2,3584]{2,1,0:T(2,128)(2,1)}, ...), branch_computations={%region_0.0_spmd, %region_1.0_spmd, %region_2.5_spmd} | conditional | flops 45102399488 | bytes 227301760
  32.5 153.1 %branch_0_fun.2 = (bf16[256,3584]{1,0:T(8,128)(2,1)}, bf16[256,3584]{1,0:T(8,128)(2,1)}, bf16[256,3584]{1,0:T(8,128)(2,1)}, f32[64,4096]{1,0:T(8,128)}, bf16[64,...) custom-call(bf16[2,288,2048]{2,1,0:T(8,128)(2,1)S(1)} %get-tuple-element.79.packed_ref.rows_ref, ...), custom_call_target="tpu_custom_call" | custom-call | flops 22548578304 | bytes 44040192 | tf_op jit(solution)/shard_map/cond/branch_0_fun/pallas_call | solution.py:492
  185.6 1.6 collective-permute-start
  187.2 1.5 collective-permute-start.1
  188.7 0.5 collective-permute-start.2
  189.2 9.1 %fusion = bf16[3584,2048]{1,0:T(8,128)(2,1)} fusion(bf16[256,3584]{1,0:T(8,128)(2,1)} %get-tuple-element.87, bf16[2,288,2048]{2,1,0:T(8,128)(2,1)S(1)} %get-tuple-element.79.packed_ref.rows_ref), kind=kOutput, calls=%fused_computation | convolution fusion | flops 3758096384 | bytes 17563648 | tf_op jit(solution)/shard_map/cond/branch_0_fun/dot_general | solution.py:17
  198.2 0.0 copy-start.5
  198.2 18.9 %branch_0_fun.3 = bf16[2048,2,3584]{2,1,0:T(2,128)(2,1)} custom-call(bf16[2,288,2048]{2,1,0:T(8,128)(2,1)S(1)} %get-tuple-element.79.packed_ref.rows_ref, bf16[256,3584]{1,0:T(8,128)(2,1)} %get-tuple-element.88.gate_ref, bf16[256,3584]{1,0:T(8,128)(2,1)} %get-tuple-element.89.up_ref), custom_call_target="tpu_custom_call" | custom-call | flops 7516192768 | bytes 35127296 | tf_op jit(solution)/shard_map/cond/branch_0_fun/pallas_call | solution.py:63
  217.2 0.0 collective-permute-done
  217.2 0.0 collective-permute-done.1
  217.2 0.0 collective-permute-done.2
  217.2 0.0 copy-done.5
  217.2 1.6 add_convert_fusion
  218.8 0.8 fusion.13
Async XLA Ops:
  185.6 31.6 %collective-permute-start = (bf16[64,4096]{1,0:T(8,128)(2,1)}, bf16[64,4096]{1,0:T(8,128)(2,1)}, u32[]{:S(2)}, u32[]{:S(2)}) collective-permute-start(bf16[64,4096]{1,0:T(8,128)(2,1)} %get-tuple-element.84), channel_id=1, source_target_pairs={{0,2},{1,3},{2,0},{3,1},{4,6},{5,7},{6,4},{7,5},{8,10},{9,11},{10,... | collective-permute-start | bytes 1572872 | tf_op jit(solution)/shard_map/cond/branch_0_fun/ppermute | solution.py:41
  187.2 30.0 %collective-permute-start.1 = (bf16[64,4096]{1,0:T(8,128)(2,1)}, bf16[64,4096]{1,0:T(8,128)(2,1)}, u32[]{:S(2)}, u32[]{:S(2)}) collective-permute-start(bf16[64,4096]{1,0:T(8,128)(2,1)} %get-tuple-element.85), channel_id=1, source_target_pairs={{0,4},{1,5},{2,6},{3,7},{4,0},{5,1},{6,2},{7,3},{8,12},{9,13},{10,... | collective-permute-start | bytes 1572872 | tf_op jit(solution)/shard_map/cond/branch_0_fun/ppermute | solution.py:41
  188.7 28.5 %collective-permute-start.2 = (bf16[64,4096]{1,0:T(8,128)(2,1)}, bf16[64,4096]{1,0:T(8,128)(2,1)}, u32[]{:S(2)}, u32[]{:S(2)}) collective-permute-start(bf16[64,4096]{1,0:T(8,128)(2,1)} %get-tuple-element.86), channel_id=1, source_target_pairs={{0,6},{1,7},{2,4},{3,5},{4,2},{5,3},{6,0},{7,1},{8,14},{9,15},{10,... | collective-permute-start | bytes 1572872 | tf_op jit(solution)/shard_map/cond/branch_0_fun/ppermute | solution.py:41
  198.2 19.0 %copy-start.5 = (f32[64,4096]{1,0:T(8,128)S(1)}, f32[64,4096]{1,0:T(8,128)}, u32[]{:S(2)}) copy-start(f32[64,4096]{1,0:T(8,128)} %get-tuple-element.83) | copy-start | bytes 3145732 | tf_op jit(solution)/shard_map/conditional
